TPU v7x, 128 devices: a whole 4x4x4 slice. The times are simulated.
128 devices in a mesh: rcv: 16 (over x_hi, y, core), src: 8 (over z, x_lo).
Axes of the slice: x: 4 (x_hi: 2, x_lo: 2; x = x_hi * 2 + x_lo), y: 4, z: 4, core: 2. Of those that a mesh axis runs over, the one named last changes fastest.
Arguments:
- kernel_codes: bfloat16 [2, 8192, 65536], P(None, 'rcv', 'src'), may hold values from -128 to 127
- kernel_exps: int32 [8192, 512], P('rcv', 'src'), may hold values from -17 to -14
- wavefield: bfloat16 [2, 65536, 128], P(None, 'src', 'rcv'), may hold values from -6 to 6
- observed: bfloat16 [2, 8192, 128], P(None, 'rcv'), may hold values from -6 to 6
- receiver_mask: int32 [8192], P('rcv'), may hold values 0 or 1
Outputs:
- residual: bfloat16 [2, 8192, 128], P(None, 'rcv', 'src')
- gradient: bfloat16 [2, 65536, 128], P(None, 'src', 'rcv')
All inputs are finite; a program needn't handle non-finite values. No bound on the sum of `receiver_mask` on one device may be relied on, other than what follows from the above.
Results may differ from a plain program's by a relative error of at most 0.0049.
Values may be sent and summed in bfloat16 or wider, within the bound.
No kernel may reach another device: no remote copies, remote signals or barrier semaphores. Data moves between devices by JAX's collectives and lax.ppermute only.
A program may use at most 128 MiB of HBM per device.

v0:
```python
import jax
import jax.numpy as jnp
from jax import lax
from jax.sharding import PartitionSpec as P

EXP_BLOCK = 128


def decode(codes, exps):
    rows = codes.shape[1]
    cols = codes.shape[2]
    scale = jnp.exp2(exps.astype(jnp.float32))[:, :, None]

    def widen(values):
        blocks = values.reshape(rows, cols // EXP_BLOCK, EXP_BLOCK).astype(jnp.float32) * scale
        return blocks.reshape(rows, cols).astype(jnp.bfloat16)

    return jnp.concatenate([widen(codes[0]), widen(codes[1])], axis=0)


def body(kernel_codes, kernel_exps, wavefield, observed, receiver_mask):
    rows = kernel_codes.shape[1]
    n_src = lax.axis_size("src")
    stacked = decode(kernel_codes, kernel_exps)
    piece = lax.all_gather(wavefield, "rcv", axis=2, tiled=True)
    span = piece.shape[2]
    joined = jnp.concatenate([piece[0], piece[1]], axis=1)
    prod = jnp.dot(stacked, joined, preferred_element_type=jnp.float32)
    pred_real = prod[:rows, :span] - prod[rows:, span:]
    pred_imag = prod[:rows, span:] + prod[rows:, :span]
    partial_pred = jnp.stack([pred_real, pred_imag])
    width = partial_pred.shape[2]
    share_cols = width // n_src
    live = receiver_mask.astype(jnp.float32)[None, :, None]
    predicted = lax.psum(partial_pred, "src")
    resid = (live * (predicted - observed.astype(jnp.float32))).astype(jnp.bfloat16)
    own_resid = lax.dynamic_slice_in_dim(resid, lax.axis_index("src") * share_cols, share_cols, 2)
    left = jnp.concatenate([resid[0], resid[1]], axis=0)
    right = jnp.concatenate([resid[1], -resid[0]], axis=0)
    grad_real = lax.dot_general(
        stacked, left, (((0,), (0,)), ((), ())), preferred_element_type=jnp.float32
    )
    grad_imag = lax.dot_general(
        stacked, right, (((0,), (0,)), ((), ())), preferred_element_type=jnp.float32
    )
    summed = lax.psum_scatter(
        jnp.stack([grad_real, grad_imag]), "rcv", scatter_dimension=2, tiled=True
    )
    gradient = summed.astype(jnp.bfloat16)
    return (own_resid, gradient)


def solution(mesh):
    in_specs = (
        P(None, "rcv", "src"),
        P("rcv", "src"),
        P(None, "src", "rcv"),
        P(None, "rcv", None),
        P("rcv"),
    )
    out_specs = (P(None, "rcv", "src"), P(None, "src", "rcv"))
    return jax.shard_map(body, mesh=mesh, in_specs=in_specs, out_specs=out_specs, check_vma=False)
```

profile of v0, /device:TPU:0, one launch (start us, length us, event | category | flops | bytes accessed | tf_op | source)
XLA Modules:
  0.0 313.3 jit_solution(1897431621627236321)
XLA Ops:
  7.2 0.7 all-gather.2.cloned.1.call-update
  7.9 0.9 multiply_exponential_fusion
  8.9 0.1 copy.10
  9.0 4.6 %mul.30 = f32[512,64,128]{2,1,0:T(8,128)S(1)} broadcast(f32[512,64]{1,0:T(8,128)S(1)} %copy.10), dimensions={0,1} | broadcast | bytes 16908288 | tf_op jit(solution)/shard_map/mul | solution.py:15
  13.6 18.3 %fusion = (bf16[512,8192]{1,0:T(8,128)(2,1)}, bf16[512,8192]{1,0:T(8,128)(2,1)}) fusion(f32[64,8,64,128]{3,2,1,0:T(8,128)S(1)} %bitcast.33, bf16[2,512,8192]{2,1,0:T(8,128)(2,1)} %param.5), kind=kLoop, calls=%fused_computation.2 | loop fusion | flops 25165824 | bytes 50331648 | tf_op jit(solution)/shard_map/convert_element_type | solution.py:16
  32.0 35.8 %all-gather.2.cloned.1.call-done = bf16[2,8192,128]{1,2,0:T(8,128)(2,1)} async-done(((bf16[2,8192,8]{1,2,0:T(8,128)(2,1)}), bf16[2,8192,128]{1,2,0:T(8,128)(2,1)}) %all-gather.2.cloned.1.call-update) | async-done | bytes 4194320 | tf_op jit(solution)/shard_map/all_gather | solution.py:25
  67.7 4.1 %slice_bitcast_fusion.1 = (bf16[8192,128]{0,1:T(8,128)(2,1)S(1)}, bf16[8192,128]{0,1:T(8,128)(2,1)}) fusion(bf16[2,8192,128]{1,2,0:T(8,128)(2,1)} %all-gather.2.cloned.1.call-done), kind=kLoop, calls=%fused_computation.13 | loop fusion | bytes 8388608 | tf_op jit(solution)/shard_map/squeeze | solution.py:27
  71.8 1.3 copy-done
  73.1 9.5 %fusion.2 = f32[1024,256]{1,0:T(8,128)} fusion(bf16[512,8192]{1,0:T(8,128)(2,1)} %get-tuple-element.7, bf16[512,8192]{1,0:T(8,128)(2,1)S(1)} %copy-done, bf16[8192,128]{0,1:T(8,128)(2,1)} %get-tuple-element.9, bf16[8192,128]{0,1:T(8,128)(2,1)S(1)} %get-tuple-element.8), kind=kOutput, calls=%fused_computation.8 | convolution fusion | flops 4336910336 | bytes 22020096 | tf_op jit(solution)/shard_map/dot_general | solution.py:28
  82.7 1.2 fusion.7
  83.9 0.8 pad_maximum_fusion.5
  84.8 0.6 dynamic-slice
  86.1 73.1 %all-reduce.4.cloned.1.call-done = f32[2,512,128]{2,1,0:T(8,128)} async-done(((f32[2,512,128]{2,1,0:T(8,128)}), f32[2,512,128]{2,1,0:T(8,128)}) %all-reduce.4.cloned.1.call-update) | async-done | bytes 524304 | tf_op jit(solution)/shard_map/psum | solution.py:35
  159.2 1.3 multiply_convert_fusion
  160.6 10.2 %convolution_bitcast_fusion.1 = f32[1,8192,128]{2,1,0:T(8,128)} fusion(bf16[512,8192]{1,0:T(8,128)(2,1)} %get-tuple-element.7, bf16[512,8192]{1,0:T(8,128)(2,1)} %get-tuple-element.6, bf16[512,128]{1,0:T(8,128)(2,1)S(1)} %get-tuple-element.13, bf16[512,128]{1,0:T(8,128)(2,1)S(1)} %get-tuple-element.12), kind=kOutput, calls=%fused_computation.6 | convolution fusion | flops 2181562368 | bytes 21233664 | tf_op jit(solution)/shard_map/dot_general | solution.py:40
  170.9 0.9 slice-done.3
  171.7 6.3 %convolution_bitcast_fusion = f32[1,8192,128]{2,1,0:T(8,128)} fusion(bf16[512,8192]{1,0:T(8,128)(2,1)S(1)} %bitcast.37, bf16[512,8192]{1,0:T(8,128)(2,1)S(1)} %bitcast.35, bf16[512,128]{1,0:T(8,128)(2,1)S(1)} %fusion.17, bf16[512,128]{1,0:T(8,128)(2,1)S(1)} %get-tuple-element.13), kind=kOutput, calls=%fused_computation.5 | convolution fusion | flops 2181562368 | bytes 21233664 | tf_op jit(solution)/shard_map/dot_general | solution.py:43
  178.0 7.2 %pad_maximum_fusion.1 = f32[2,8192,128]{2,1,0:T(8,128)} fusion(f32[1,8192,128]{2,1,0:T(8,128)} %convolution_bitcast_fusion, f32[1,8192,128]{2,1,0:T(8,128)} %convolution_bitcast_fusion.1), kind=kLoop, calls=%fused_computation.7 | loop fusion | flops 2097152 | bytes 16777216 | tf_op jit(solution)/shard_map/stack | solution.py:47
  185.2 13.2 %copy.11 = f32[2,8192,128]{1,0,2:T(2,128)} copy(f32[2,8192,128]{2,1,0:T(8,128)} %pad_maximum_fusion.1) | data formatting | bytes 16777216 | tf_op jit(solution)/shard_map/stack | solution.py:47
  198.4 105.1 %all-reduce.5 = bf16[2,8192,128]{1,0,2:T(2,128)(2,1)} all-reduce(f32[2,8192,128]{1,0,2:T(2,128)} %copy.11), channel_id=2, replica_groups=mesh['rcv'=16,'src'=8] {'rcv'}, use_global_device_ids=true, to_apply=%region_1.0.clone | all-reduce | flops 2097152 | bytes 12582912
  303.6 1.1 dynamic-slice_convert_fusion
  304.7 0.9 copy.13
  305.6 0.1 constant_dynamic-slice_fusion
  305.7 0.7 copy.12
  (22 shorter events, 0.2 us)
Async XLA Ops:
  7.2 60.6 %all-gather.2.cloned.1.call-start = ((), (), s32[]{:S(2)}) async-start(), calls=%async_computation | async-start | bytes 4456448 | tf_op jit(solution)/shard_map/all_gather | solution.py:25
  7.9 151.3 %all-reduce.4.cloned.1.call-start = ((), (), s32[]{:S(2)}) async-start(), calls=%async_computation.1 | async-start | bytes 1048576 | tf_op jit(solution)/shard_map/psum | solution.py:35
  67.7 5.4 %copy-start = (bf16[512,8192]{1,0:T(8,128)(2,1)S(1)}, bf16[512,8192]{1,0:T(8,128)(2,1)}, u32[]{:S(2)}) copy-start(bf16[512,8192]{1,0:T(8,128)(2,1)} %get-tuple-element.6) | copy-start | bytes 25165828
  73.1 11.7 %copy-start.2 = (s32[512]{0:T(512)S(1)}, s32[512]{0:T(512)}, u32[]{:S(2)}) copy-start(s32[512]{0:T(512)} %param.9) | copy-start | bytes 6148
  73.1 11.7 %copy-start.3 = (u32[128]{0:T(128)S(1)}, u32[128]{0:T(128)}, u32[]{:S(2)}) copy-start(u32[128]{0:T(128)} %constant.15) | copy-start | bytes 1540
  73.1 86.1 %copy-start.1 = (bf16[2,512,128]{2,1,0:T(8,128)(2,1)S(1)}, bf16[2,512,128]{2,1,0:T(8,128)(2,1)}, u32[]{:S(2)}) copy-start(bf16[2,512,128]{2,1,0:T(8,128)(2,1)} %param.8) | copy-start | bytes 786436
  159.2 11.6 %slice-start = ((s8[8388608]{0:T(1024)(128)(4,1)}), s8[4194304]{0:T(1024)(128)(4,1)S(1)}, s32[]{:S(2)}) async-start(s8[8388608]{0:T(1024)(128)(4,1)} %bitcast.34), calls=%async_computation.2 | async-start | bytes 8388608
  159.2 11.6 %slice-start.2 = ((s8[8388608]{0:T(1024)(128)(4,1)}), s8[4194304]{0:T(1024)(128)(4,1)S(1)}, s32[]{:S(2)}) async-start(s8[8388608]{0:T(1024)(128)(4,1)} %bitcast.36), calls=%async_computation.4 | async-start | bytes 8388608
  160.6 10.3 %slice-start.1 = ((s8[8388608]{0:T(1024)(128)(4,1)}), s8[4194304]{0:T(1024)(128)(4,1)S(1)}, s32[]{:S(2)}) async-start(s8[8388608]{0:T(1024)(128)(4,1)} %bitcast.34), calls=%async_computation.3 | async-start | bytes 8388608
  160.6 11.1 %slice-start.3 = ((s8[8388608]{0:T(1024)(128)(4,1)}), s8[4194304]{0:T(1024)(128)(4,1)S(1)}, s32[]{:S(2)}) async-start(s8[8388608]{0:T(1024)(128)(4,1)} %bitcast.36), calls=%async_computation.5 | async-start | bytes 8388608
Sparse Core Ops, SparseCore 0:
  10.5 57.1 all-gather.1
  84.9 74.2 all-reduce.3
where the time goes:
time: 314 us; the launch traced here: 313 us
  waiting for transfers between devices  110 us (35%)
  blocking collectives  105 us (33%)
  other arithmetic  29.9 us (10%)
  local copies, waits for them, and re-layouts  27.7 us (9%)
  matrix products  26 us (8%)
  between operations  14.8 us (5%)
    unnamed x1, blocking collectives  105 us
    psum x1, waiting for transfers between devices, body(): predicted = lax.psum(partial_pred, 'src')  73.1 us
    all_gather x1, waiting for transfers between devices, body(): piece = lax.all_gather(wavefield, 'rcv', axis=2, tiled=True)  35.8 us
    convert_element_type x1, other arithmetic, widen(): return blocks.reshape(rows, cols).astype(jnp.bfloat16)  18.3 us
    another operation x1, local copies, waits for them, and re-layouts, body(): jnp.stack([grad_real, grad_imag])  13.2 us
    dot_general x1, matrix products, body(): lax.dot_general(stacked, left, (((0,), (0,)), ((), ())), preferred_elemen...  10.2 us
    dot_general x1, matrix products, body(): prod = jnp.dot(stacked, joined, preferred_element_type=jnp.float32)  9.54 us
    another operation x1, other arithmetic, body(): jnp.stack([grad_real, grad_imag])  7.24 us
  transfers between devices with their start and end apart: 2, of which 2 were waited for; matrix products, arithmetic and copies ran while one was open for 8% of the time, Pallas kernels for 0%

commit v1 on v0

--- a/solution.py
+++ b/solution.py
@@ -32,7 +32,7 @@
     width = partial_pred.shape[2]
     share_cols = width // n_src
     live = receiver_mask.astype(jnp.float32)[None, :, None]
-    predicted = lax.psum(partial_pred, "src")
+    predicted = jnp.sum(lax.all_gather(partial_pred, "src"), axis=0)
     resid = (live * (predicted - observed.astype(jnp.float32))).astype(jnp.bfloat16)
     own_resid = lax.dynamic_slice_in_dim(resid, lax.axis_index("src") * share_cols, share_cols, 2)
     left = jnp.concatenate([resid[0], resid[1]], axis=0)

time: 314 us -> 332 us (1.057)
  waiting for transfers between devices: 110 us -> 124 us
    all_gather x0 -> x1, waiting for transfers between devices: none -> 87.7 us  [body(): predicted = jnp.sum(lax.all_gather(partial_pred, 'src'), axis=0)]
    psum x1 -> x0, waiting for transfers between devices: 73.1 us -> none  [body(): predicted = lax.psum(partial_pred, 'src')]
  transfers between devices with their start and end apart: 2 -> 2, of which waited for: 2 -> 2; matrix products, arithmetic and copies ran while one was open for 8% -> 7% of each run, Pallas kernels for 0% -> 0%
where the time goes in v1:
time: 332 us; the launch traced here: 331 us
  waiting for transfers between devices  124 us (37%)
  blocking collectives  106 us (32%)
  other arithmetic  31.2 us (9%)
  local copies, waits for them, and re-layouts  28.9 us (9%)
  matrix products  25.8 us (8%)
  between operations  14.8 us (4%)
    unnamed x1, blocking collectives  106 us
    all_gather x1, waiting for transfers between devices, body(): predicted = jnp.sum(lax.all_gather(partial_pred, 'src'), axis=0)  87.7 us
    all_gather x1, waiting for transfers between devices, body(): piece = lax.all_gather(wavefield, 'rcv', axis=2, tiled=True)  35.8 us
    convert_element_type x1, other arithmetic, widen(): return blocks.reshape(rows, cols).astype(jnp.bfloat16)  18.3 us
    another operation x1, local copies, waits for them, and re-layouts, body(): jnp.stack([grad_real, grad_imag])  13.2 us
    dot_general x1, matrix products, body(): lax.dot_general(stacked, left, (((0,), (0,)), ((), ())), preferred_elemen...  9.97 us
    dot_general x1, matrix products, body(): prod = jnp.dot(stacked, joined, preferred_element_type=jnp.float32)  9.54 us
    another operation x1, other arithmetic, body(): jnp.stack([grad_real, grad_imag])  7.24 us
  transfers between devices with their start and end apart: 2, of which 2 were waited for; matrix products, arithmetic and copies ran while one was open for 7% of the time, Pallas kernels for 0%

profile of v1, /device:TPU:0, one launch (start us, length us, event | category | flops | bytes accessed | tf_op | source)
XLA Modules:
  0.0 331.0 jit_solution(6209952137003832848)
XLA Ops:
  7.2 0.7 all-gather.4.cloned.1.call-update
  7.9 0.9 multiply_exponential_fusion
  9.0 4.6 %mul.30 = f32[512,64,128]{2,1,0:T(8,128)S(1)} broadcast(f32[512,64]{1,0:T(8,128)S(1)} %copy.10), dimensions={0,1} | broadcast | bytes 16908288 | tf_op jit(solution)/shard_map/mul | solution.py:15
  13.6 18.3 %fusion = (bf16[512,8192]{1,0:T(8,128)(2,1)}, bf16[512,8192]{1,0:T(8,128)(2,1)}) fusion(f32[64,8,64,128]{3,2,1,0:T(8,128)S(1)} %bitcast.34, bf16[2,512,8192]{2,1,0:T(8,128)(2,1)} %param.5), kind=kLoop, calls=%fused_computation.2 | loop fusion | flops 25165824 | bytes 50331648 | tf_op jit(solution)/shard_map/convert_element_type | solution.py:16
  32.0 35.8 %all-gather.4.cloned.1.call-done = bf16[2,8192,128]{1,2,0:T(8,128)(2,1)} async-done(((bf16[2,8192,8]{1,2,0:T(8,128)(2,1)}), bf16[2,8192,128]{1,2,0:T(8,128)(2,1)}) %all-gather.4.cloned.1.call-update) | async-done | bytes 4194320 | tf_op jit(solution)/shard_map/all_gather | solution.py:25
  67.7 4.1 %slice_bitcast_fusion.1 = (bf16[8192,128]{0,1:T(8,128)(2,1)S(1)}, bf16[8192,128]{0,1:T(8,128)(2,1)}) fusion(bf16[2,8192,128]{1,2,0:T(8,128)(2,1)} %all-gather.4.cloned.1.call-done), kind=kLoop, calls=%fused_computation.13 | loop fusion | bytes 8388608 | tf_op jit(solution)/shard_map/squeeze | solution.py:27
  71.8 1.3 copy-done
  73.1 9.5 %fusion.2 = f32[1024,256]{1,0:T(8,128)} fusion(bf16[512,8192]{1,0:T(8,128)(2,1)} %get-tuple-element.7, bf16[512,8192]{1,0:T(8,128)(2,1)S(1)} %copy-done, bf16[8192,128]{0,1:T(8,128)(2,1)} %get-tuple-element.9, bf16[8192,128]{0,1:T(8,128)(2,1)S(1)} %get-tuple-element.8), kind=kOutput, calls=%fused_computation.8 | convolution fusion | flops 4336910336 | bytes 22020096 | tf_op jit(solution)/shard_map/dot_general | solution.py:28
  82.7 1.2 fusion.7
  83.9 0.8 pad_maximum_fusion.5
  84.8 0.6 dynamic-slice
  86.1 87.7 %all-gather.6.cloned.1.call-done = f32[16,512,128]{2,1,0:T(8,128)} async-done(((f32[2,512,128]{2,1,0:T(8,128)}), f32[16,512,128]{2,1,0:T(8,128)}) %all-gather.6.cloned.1.call-update) | async-done | bytes 4194320 | tf_op jit(solution)/shard_map/all_gather | solution.py:35
  173.8 2.4 reduce_sum.9
  176.3 0.1 multiply_convert_fusion
  176.5 10.0 %convolution_bitcast_fusion.1 = f32[1,8192,128]{2,1,0:T(8,128)} fusion(bf16[512,8192]{1,0:T(8,128)(2,1)} %get-tuple-element.7, bf16[512,8192]{1,0:T(8,128)(2,1)} %get-tuple-element.6, bf16[512,128]{1,0:T(8,128)(2,1)S(1)} %get-tuple-element.13, bf16[512,128]{1,0:T(8,128)(2,1)S(1)} %get-tuple-element.12), kind=kOutput, calls=%fused_computation.6 | convolution fusion | flops 2181562368 | bytes 21233664 | tf_op jit(solution)/shard_map/dot_general | solution.py:40
  186.5 0.8 slice-done.1
  187.3 1.2 slice-done.3
  188.5 6.3 %convolution_bitcast_fusion = f32[1,8192,128]{2,1,0:T(8,128)} fusion(bf16[512,8192]{1,0:T(8,128)(2,1)S(1)} %bitcast.38, bf16[512,8192]{1,0:T(8,128)(2,1)S(1)} %bitcast.36, bf16[512,128]{1,0:T(8,128)(2,1)S(1)} %fusion.17, bf16[512,128]{1,0:T(8,128)(2,1)S(1)} %get-tuple-element.13), kind=kOutput, calls=%fused_computation.5 | convolution fusion | flops 2181562368 | bytes 21233664 | tf_op jit(solution)/shard_map/dot_general | solution.py:43
  194.8 7.2 %pad_maximum_fusion.1 = f32[2,8192,128]{2,1,0:T(8,128)} fusion(f32[1,8192,128]{2,1,0:T(8,128)} %convolution_bitcast_fusion, f32[1,8192,128]{2,1,0:T(8,128)} %convolution_bitcast_fusion.1), kind=kLoop, calls=%fused_computation.7 | loop fusion | flops 2097152 | bytes 16777216 | tf_op jit(solution)/shard_map/stack | solution.py:47
  202.0 13.2 %copy.11 = f32[2,8192,128]{1,0,2:T(2,128)} copy(f32[2,8192,128]{2,1,0:T(8,128)} %pad_maximum_fusion.1) | data formatting | bytes 16777216 | tf_op jit(solution)/shard_map/stack | solution.py:47
  215.3 106.0 %all-reduce.2 = bf16[2,8192,128]{1,0,2:T(2,128)(2,1)} all-reduce(f32[2,8192,128]{1,0,2:T(2,128)} %copy.11), channel_id=3, replica_groups=mesh['rcv'=16,'src'=8] {'rcv'}, use_global_device_ids=true, to_apply=%region_1.0.clone | all-reduce | flops 2097152 | bytes 12582912
  321.3 1.1 dynamic-slice_convert_fusion
  322.4 0.9 copy.13
  323.4 0.7 copy.12
  (23 shorter events, 0.4 us)
Async XLA Ops:
  7.2 60.6 %all-gather.4.cloned.1.call-start = ((), (), s32[]{:S(2)}) async-start(), calls=%async_computation | async-start | bytes 4456448 | tf_op jit(solution)/shard_map/all_gather | solution.py:25
  7.9 165.9 %all-gather.6.cloned.1.call-start = ((), (), s32[]{:S(2)}) async-start(), calls=%async_computation.1 | async-start | bytes 4718592 | tf_op jit(solution)/shard_map/all_gather | solution.py:35
  67.7 5.4 %copy-start = (bf16[512,8192]{1,0:T(8,128)(2,1)S(1)}, bf16[512,8192]{1,0:T(8,128)(2,1)}, u32[]{:S(2)}) copy-start(bf16[512,8192]{1,0:T(8,128)(2,1)} %get-tuple-element.6) | copy-start | bytes 25165828
  73.1 11.7 %copy-start.2 = (s32[512]{0:T(512)S(1)}, s32[512]{0:T(512)}, u32[]{:S(2)}) copy-start(s32[512]{0:T(512)} %param.9) | copy-start | bytes 6148
  73.1 11.7 %copy-start.3 = (u32[128]{0:T(128)S(1)}, u32[128]{0:T(128)}, u32[]{:S(2)}) copy-start(u32[128]{0:T(128)} %constant.17) | copy-start | bytes 1540
  73.1 103.1 %copy-start.1 = (bf16[2,512,128]{2,1,0:T(8,128)(2,1)S(1)}, bf16[2,512,128]{2,1,0:T(8,128)(2,1)}, u32[]{:S(2)}) copy-start(bf16[2,512,128]{2,1,0:T(8,128)(2,1)} %param.8) | copy-start | bytes 786436
  176.3 10.2 %slice-start = ((s8[8388608]{0:T(1024)(128)(4,1)}), s8[4194304]{0:T(1024)(128)(4,1)S(1)}, s32[]{:S(2)}) async-start(s8[8388608]{0:T(1024)(128)(4,1)} %bitcast.35), calls=%async_computation.2 | async-start | bytes 8388608
  176.3 10.2 %slice-start.2 = ((s8[8388608]{0:T(1024)(128)(4,1)}), s8[4194304]{0:T(1024)(128)(4,1)S(1)}, s32[]{:S(2)}) async-start(s8[8388608]{0:T(1024)(128)(4,1)} %bitcast.37), calls=%async_computation.4 | async-start | bytes 8388608
  176.5 10.8 %slice-start.1 = ((s8[8388608]{0:T(1024)(128)(4,1)}), s8[4194304]{0:T(1024)(128)(4,1)S(1)}, s32[]{:S(2)}) async-start(s8[8388608]{0:T(1024)(128)(4,1)} %bitcast.35), calls=%async_computation.3 | async-start | bytes 8388608
  176.5 12.0 %slice-start.3 = ((s8[8388608]{0:T(1024)(128)(4,1)}), s8[4194304]{0:T(1024)(128)(4,1)S(1)}, s32[]{:S(2)}) async-start(s8[8388608]{0:T(1024)(128)(4,1)} %bitcast.37), calls=%async_computation.5 | async-start | bytes 8388608
Sparse Core Ops, SparseCore 0:
  10.5 57.1 all-gather.3
  84.9 88.8 all-gather.5
